TPU v7x, 32 devices: a whole 2x2x4 slice. The times are simulated.
32 devices in a mesh: dp: 8 (over z, x), rep: 4 (over y, core).
Axes of the slice: x: 2, y: 2, z: 4, core: 2. Of those that a mesh axis runs over, the one named last changes fastest.
Arguments:
- tokens: bfloat16 [128, 256, 512], P(('dp', 'rep')), may hold values from -6 to 6
- cotangent: bfloat16 [128, 256, 512], P(('dp', 'rep')), may hold values from -6 to 6
- target_lengths: int32 [128], P(('dp', 'rep')), may hold values from 32 to 256, as said below
- task_mask: int32 [128, 256], P(('dp', 'rep')), may hold values 0 or 1
- memory_lengths: int32 [128], P(('dp', 'rep')), may hold values from 256 to 1024, as said below
- position_buckets: int32 [256, 256], replicated, may hold values from 0 to 510
- memory: bfloat16 [8, 16, 1024, 512], P(None, 'rep', 'dp'), may hold values from -6 to 6
- self_gain: float32 [512], replicated, may hold values from 0.25 to 1.75
- self_shift: float32 [512], replicated, may hold values from -1.75 to 1.75
- query_weight: bfloat16 [512, 512], replicated, may hold values from -0.25 to 0.25
- query_bias: float32 [512], replicated, may hold values from -1.75 to 1.75
- key_weight: bfloat16 [512, 512], replicated, may hold values from -0.25 to 0.25
- value_weight: bfloat16 [512, 512], replicated, may hold values from -0.25 to 0.25
- value_bias: float32 [512], replicated, may hold values from -1.75 to 1.75
- position_table: float32 [511, 8], replicated, may hold values from -6 to 6
- head_scale: float32 [8], replicated, may hold values from 0.5 to 1.5
- output_weight: bfloat16 [512, 512], replicated, may hold values from -1 to 1
- output_bias: float32 [512], replicated, may hold values from -1.75 to 1.75
- cross_gain: float32 [512], replicated, may hold values from 0.25 to 1.75
- cross_shift: float32 [512], replicated, may hold values from -1.75 to 1.75
- cross_query: bfloat16 [512, 512], replicated, may hold values from -0.25 to 0.25
- cross_query_bias: float32 [512], replicated, may hold values from -1.75 to 1.75
- cross_key: bfloat16 [512, 512], replicated, may hold values from -0.25 to 0.25
- cross_value: bfloat16 [512, 512], replicated, may hold values from -0.25 to 0.25
- cross_value_bias: float32 [512], replicated, may hold values from -1.75 to 1.75
- post_gain: float32 [512], replicated, may hold values from 0.25 to 1.75
- post_shift: float32 [512], replicated, may hold values from -1.75 to 1.75
- cross_output: bfloat16 [512, 512], replicated, may hold values from -0.25 to 0.25
- cross_output_bias: float32 [512], replicated, may hold values from -1.75 to 1.75
- feed_gain: float32 [512], replicated, may hold values from 0.25 to 1.75
- feed_shift: float32 [512], replicated, may hold values from -1.75 to 1.75
- inner_weight: bfloat16 [512, 2048], replicated, may hold values from -0.25 to 0.25
- inner_bias: float32 [2048], replicated, may hold values from -1.75 to 1.75
- inner_gain: float32 [2048], replicated, may hold values from 0.25 to 1.75
- inner_shift: float32 [2048], replicated, may hold values from -1.75 to 1.75
- outer_weight: bfloat16 [2048, 512], replicated, may hold values from -0.125 to 0.125
- outer_bias: float32 [512], replicated, may hold values from -1.75 to 1.75
Outputs:
- layer_output: bfloat16 [128, 256, 512], P(('dp', 'rep'))
- tokens_gradient: bfloat16 [128, 256, 512], P(('dp', 'rep'))
- memory_gradient: bfloat16 [8, 16, 1024, 512], P(None, 'rep', 'dp')
- gradient_self_gain: float32 [512], replicated
- gradient_self_shift: float32 [512], replicated
- gradient_query_weight: float32 [512, 512], replicated
- gradient_query_bias: float32 [512], replicated
- gradient_key_weight: float32 [512, 512], replicated
- gradient_value_weight: float32 [512, 512], replicated
- gradient_value_bias: float32 [512], replicated
- gradient_position_table: float32 [511, 8], replicated
- gradient_head_scale: float32 [8], replicated
- gradient_output_weight: float32 [512, 512], replicated
- gradient_output_bias: float32 [512], replicated
- gradient_cross_gain: float32 [512], replicated
- gradient_cross_shift: float32 [512], replicated
- gradient_cross_query: float32 [512, 512], replicated
- gradient_cross_query_bias: float32 [512], replicated
- gradient_cross_key: float32 [512, 512], replicated
- gradient_cross_value: float32 [512, 512], replicated
- gradient_cross_value_bias: float32 [512], replicated
- gradient_post_gain: float32 [512], replicated
- gradient_post_shift: float32 [512], replicated
- gradient_cross_output: float32 [512, 512], replicated
- gradient_cross_output_bias: float32 [512], replicated
- gradient_feed_gain: float32 [512], replicated
- gradient_feed_shift: float32 [512], replicated
- gradient_inner_weight: float32 [512, 2048], replicated
- gradient_inner_bias: float32 [2048], replicated
- gradient_inner_gain: float32 [2048], replicated
- gradient_inner_shift: float32 [2048], replicated
- gradient_outer_weight: float32 [2048, 512], replicated
- gradient_outer_bias: float32 [512], replicated
Inputs may be any that keep to these rules, and one draw needn't show every extreme that they name: `target_lengths`: some sequence has 256 real tokens in every draw; later positions are padding. `memory_lengths`: some sequence has all 1024 memory positions real in every draw.
All inputs are finite; a program needn't handle non-finite values. No bound on the sum of `task_mask` on one device may be relied on, other than what follows from the above.
Results may differ from a plain program's by a relative error of at most 0.017.
Values may be sent and summed in bfloat16 or wider, within the bound.
A program may use at most 192 MiB of HBM per device.

v0:
```python
import jax
import jax.numpy as jnp
from jax import lax
from jax.sharding import PartitionSpec as P

big_negative = -1e30


def layer_norm(value_in, norm_gain, norm_shift):
    center = value_in - jnp.mean(value_in, axis=-1, keepdims=True)
    spread = jnp.mean(center * center, axis=-1, keepdims=True)
    return center * lax.rsqrt(spread + 1e-05) * norm_gain + norm_shift


def gelu_exact(value_in):
    return jax.nn.gelu(value_in, approximate=False)


def matmul(left_side, right_side):
    return jnp.dot(left_side, right_side, preferred_element_type=jnp.float32)


def outer_sum(left_side, right_side):
    return lax.dot_general(
        left_side, right_side, (((0,), (0,)), ((), ())), preferred_element_type=jnp.float32
    )


def back_product(grad_in, weight):
    return lax.dot_general(
        grad_in, weight, (((grad_in.ndim - 1,), (1,)), ((), ())), preferred_element_type=jnp.float32
    )


def split_heads(matrix, head_count, seq_count, span):
    return matrix.reshape(seq_count, span, head_count, -1).transpose(2, 0, 1, 3)


def merge_heads(stacked):
    head_count, seq_count, span, head_size = stacked.shape
    return stacked.transpose(1, 2, 0, 3).reshape(seq_count * span, head_count * head_size)


def bucket_blocks(position_buckets):
    length = position_buckets.shape[0]
    row_block = 64
    return position_buckets.reshape(length // row_block, row_block, length)


def scores_of(query_block, key_block, extra_bias, allowed):
    raw_scores = (
        jnp.einsum("sqd,skd->sqk", query_block, key_block, preferred_element_type=jnp.float32)
        + extra_bias
    )
    return jnp.where(allowed, raw_scores, big_negative)


def attend_forward(query_block, key_block, value_block, extra_bias, allowed):
    scores = scores_of(query_block, key_block, extra_bias, allowed)
    row_top = jnp.max(scores, axis=-1, keepdims=True)
    weights = jnp.exp(scores - row_top)
    row_total = jnp.sum(weights, axis=-1, keepdims=True)
    rounded = (weights / row_total).astype(jnp.bfloat16)
    attended = jnp.einsum("sqk,skd->sqd", rounded, value_block, preferred_element_type=jnp.float32)
    return (attended, (row_top + jnp.log(row_total))[..., 0])


def attend_backward(query_block, key_block, value_block, extra_bias, allowed, logsum, upstream):
    scores = scores_of(query_block, key_block, extra_bias, allowed)
    weights = jnp.exp(scores - logsum[..., None])
    grad_weights = jnp.einsum(
        "sqd,skd->sqk", upstream, value_block, preferred_element_type=jnp.float32
    )
    row_inner = jnp.sum(weights * grad_weights, axis=-1, keepdims=True)
    dscores = (weights * (grad_weights - row_inner)).astype(jnp.bfloat16)
    dquery = jnp.einsum("sqk,skd->sqd", dscores, key_block, preferred_element_type=jnp.float32)
    grad_keys = jnp.einsum("sqk,sqd->skd", dscores, query_block, preferred_element_type=jnp.float32)
    dvalues = jnp.einsum(
        "sqk,sqd->skd", weights.astype(jnp.bfloat16), upstream, preferred_element_type=jnp.float32
    )
    return (dquery, grad_keys, dvalues, jnp.sum(dscores.astype(jnp.float32), axis=0))


def local(
    tokens,
    cotangent,
    target_lengths,
    task_mask,
    memory_lengths,
    position_buckets,
    memory,
    self_gain,
    self_shift,
    query_weight,
    query_bias,
    key_weight,
    value_weight,
    value_bias,
    position_table,
    head_scale,
    output_weight,
    output_bias,
    cross_gain,
    cross_shift,
    cross_query,
    cross_query_bias,
    cross_key,
    cross_value,
    cross_value_bias,
    post_gain,
    post_shift,
    cross_output,
    cross_output_bias,
    feed_gain,
    feed_shift,
    inner_weight,
    inner_bias,
    inner_gain,
    inner_shift,
    outer_weight,
    outer_bias,
):
    seq_count = tokens.shape[0]
    length = tokens.shape[1]
    model_width = tokens.shape[2]
    head_count = head_scale.shape[0]
    bucket_count = position_table.shape[0]
    row_count = seq_count * length
    mem_total = memory.shape[2] * lax.axis_size("dp")
    bucket_ids = jnp.arange(bucket_count, dtype=jnp.int32)
    bucket_rows = bucket_blocks(position_buckets)
    local_key = matmul(memory, cross_key).astype(jnp.bfloat16)
    local_value = (matmul(memory, cross_value) + cross_value_bias).astype(jnp.bfloat16)
    key_arrived, value_arrived = (
        lax.all_to_all(local_key, "dp", split_axis=0, concat_axis=2, tiled=True),
        lax.all_to_all(local_value, "dp", split_axis=0, concat_axis=2, tiled=True),
    )
    key_two = key_arrived.reshape(seq_count * mem_total, model_width)
    value_two = value_arrived.reshape(seq_count * mem_total, model_width)
    places = jnp.arange(length)
    causal = places[None, :, None] >= places[None, None, :]
    self_allowed = causal & (places[None, None, :] < target_lengths[:, None, None])
    cross_allowed = jnp.arange(mem_total)[None, None, :] < memory_lengths[:, None, None]
    stream_zero = tokens.astype(jnp.float32).reshape(row_count, model_width)
    normed_one, norm_one_back = jax.vjp(layer_norm, stream_zero, self_gain, self_shift)
    normed_one_low = normed_one.astype(jnp.bfloat16)
    query_one = ((matmul(normed_one_low, query_weight) + query_bias) * 0.125).astype(jnp.bfloat16)
    key_one = matmul(normed_one_low, key_weight).astype(jnp.bfloat16)
    value_one = (matmul(normed_one_low, value_weight) + value_bias).astype(jnp.bfloat16)

    def bias_rows(rows_ids):
        one_hot = (rows_ids[:, :, None] == bucket_ids[None, None, :]).astype(jnp.float32)
        return jnp.einsum("qkb,bh->hqk", one_hot, position_table, precision=lax.Precision.HIGHEST)

    bias_heads = jnp.transpose(lax.map(bias_rows, bucket_rows), (1, 0, 2, 3)).reshape(
        head_count, length, length
    )
    heads_query = split_heads(query_one, head_count, seq_count, length)
    heads_key = split_heads(key_one, head_count, seq_count, length)
    heads_value = split_heads(value_one, head_count, seq_count, length)

    def self_forward(packed):
        return attend_forward(packed[0], packed[1], packed[2], packed[3], self_allowed)

    out_one, logsum_one = lax.map(self_forward, (heads_query, heads_key, heads_value, bias_heads))
    mixed_one = merge_heads(out_one * head_scale[:, None, None, None]).astype(jnp.bfloat16)
    stream_one = stream_zero + matmul(mixed_one, output_weight) + output_bias
    normed_two, norm_two_back = jax.vjp(layer_norm, stream_one, cross_gain, cross_shift)
    normed_two_low = normed_two.astype(jnp.bfloat16)
    query_two = ((matmul(normed_two_low, cross_query) + cross_query_bias) * 0.125).astype(
        jnp.bfloat16
    )
    heads_query_two = split_heads(query_two, head_count, seq_count, length)
    heads_key_two = split_heads(key_two, head_count, seq_count, mem_total)
    heads_value_two = split_heads(value_two, head_count, seq_count, mem_total)

    def cross_forward(packed):
        return attend_forward(packed[0], packed[1], packed[2], 0.0, cross_allowed)

    out_two, logsum_two = lax.map(cross_forward, (heads_query_two, heads_key_two, heads_value_two))
    post_two, post_back = jax.vjp(layer_norm, merge_heads(out_two), post_gain, post_shift)
    post_low = post_two.astype(jnp.bfloat16)
    stream_two = stream_one + matmul(post_low, cross_output) + cross_output_bias
    normed_three, norm_three_back = jax.vjp(layer_norm, stream_two, feed_gain, feed_shift)
    normed_three_low = normed_three.astype(jnp.bfloat16)
    inner_pre = matmul(normed_three_low, inner_weight) + inner_bias
    activated, gelu_back = jax.vjp(gelu_exact, inner_pre)
    normed_inner, inner_back = jax.vjp(layer_norm, activated, inner_gain, inner_shift)
    normed_inner_low = normed_inner.astype(jnp.bfloat16)
    stream_three = stream_two + matmul(normed_inner_low, outer_weight) + outer_bias
    layer_output = stream_three.astype(jnp.bfloat16).reshape(seq_count, length, model_width)
    keep = task_mask.astype(jnp.float32) * (places[None, :] < target_lengths[:, None]).astype(
        jnp.float32
    )
    grad_three = (cotangent.astype(jnp.float32) * keep[:, :, None]).reshape(row_count, model_width)
    sum_outer_bias = jnp.sum(grad_three, axis=0)
    low_three = grad_three.astype(jnp.bfloat16)
    sum_outer_weight = outer_sum(normed_inner_low, low_three)
    grad_activated, sum_inner_gain, sum_inner_shift = inner_back(
        back_product(low_three, outer_weight)
    )
    grad_inner = gelu_back(grad_activated)[0]
    sum_inner_bias = jnp.sum(grad_inner, axis=0)
    low_inner = grad_inner.astype(jnp.bfloat16)
    sum_inner_weight = outer_sum(normed_three_low, low_inner)
    part_two, sum_feed_gain, sum_feed_shift = norm_three_back(back_product(low_inner, inner_weight))
    grad_two = grad_three + part_two
    sum_cross_output_bias = jnp.sum(grad_two, axis=0)
    low_two = grad_two.astype(jnp.bfloat16)
    sum_cross_output = outer_sum(post_low, low_two)
    grad_merged, sum_post_gain, sum_post_shift = post_back(back_product(low_two, cross_output))
    upstream_two = split_heads(grad_merged.astype(jnp.bfloat16), head_count, seq_count, length)

    def cross_backward(packed):
        return attend_backward(
            packed[0], packed[1], packed[2], 0.0, cross_allowed, packed[3], packed[4]
        )

    dquery_two, dkey_two, dvalue_two, unused_bias = lax.map(
        cross_backward, (heads_query_two, heads_key_two, heads_value_two, logsum_two, upstream_two)
    )
    low_query_two = merge_heads(dquery_two).astype(jnp.bfloat16) * 0.125
    low_key_two = merge_heads(dkey_two).astype(jnp.bfloat16)
    low_value_two = merge_heads(dvalue_two).astype(jnp.bfloat16)
    sum_cross_query = outer_sum(normed_two_low, low_query_two)
    sum_cross_query_bias = jnp.sum(low_query_two.astype(jnp.float32), axis=0)
    sum_cross_value_bias = jnp.sum(low_value_two.astype(jnp.float32), axis=0)
    key_back, value_back = (
        lax.all_to_all(
            low_key_two.reshape(1, seq_count, mem_total, model_width),
            "dp",
            split_axis=2,
            concat_axis=0,
            tiled=True,
        ),
        lax.all_to_all(
            low_value_two.reshape(1, seq_count, mem_total, model_width),
            "dp",
            split_axis=2,
            concat_axis=0,
            tiled=True,
        ),
    )
    memory_gradient = (
        back_product(key_back, cross_key) + back_product(value_back, cross_value)
    ).astype(jnp.bfloat16)
    sum_cross_key = lax.dot_general(
        memory, key_back, (((0, 1, 2), (0, 1, 2)), ((), ())), preferred_element_type=jnp.float32
    )
    sum_cross_value = lax.dot_general(
        memory, value_back, (((0, 1, 2), (0, 1, 2)), ((), ())), preferred_element_type=jnp.float32
    )
    part_one, sum_cross_gain, sum_cross_shift = norm_two_back(
        back_product(low_query_two, cross_query)
    )
    grad_one = grad_two + part_one
    sum_output_bias = jnp.sum(grad_one, axis=0)
    low_one = grad_one.astype(jnp.bfloat16)
    sum_output_weight = outer_sum(mixed_one, low_one)
    grad_mixed = split_heads(back_product(low_one, output_weight), head_count, seq_count, length)
    sum_head_scale = jnp.sum(out_one * grad_mixed, axis=(1, 2, 3))
    upstream_one = (grad_mixed * head_scale[:, None, None, None]).astype(jnp.bfloat16)

    def self_backward(packed):
        return attend_backward(
            packed[0], packed[1], packed[2], packed[3], self_allowed, packed[4], packed[5]
        )

    dquery_one, dkey_one, dvalue_one, bias_grads = lax.map(
        self_backward, (heads_query, heads_key, heads_value, bias_heads, logsum_one, upstream_one)
    )
    block_count = bucket_rows.shape[0]
    grad_blocks = jnp.transpose(
        bias_grads.reshape(head_count, block_count, length // block_count, length), (1, 0, 2, 3)
    )

    def bucket_sums(total, packed):
        one_hot = (packed[0][:, :, None] == bucket_ids[None, None, :]).astype(jnp.float32)
        return (
            total + jnp.einsum("qkb,hqk->bh", one_hot, packed[1], precision=lax.Precision.HIGHEST),
            None,
        )

    sum_position_table, unused_end = lax.scan(
        bucket_sums, jnp.zeros((bucket_count, head_count), jnp.float32), (bucket_rows, grad_blocks)
    )
    low_query_one = merge_heads(dquery_one).astype(jnp.bfloat16) * 0.125
    low_key_one = merge_heads(dkey_one).astype(jnp.bfloat16)
    low_value_one = merge_heads(dvalue_one).astype(jnp.bfloat16)
    sum_query_weight = outer_sum(normed_one_low, low_query_one)
    sum_query_bias = jnp.sum(low_query_one.astype(jnp.float32), axis=0)
    sum_key_weight = outer_sum(normed_one_low, low_key_one)
    sum_value_weight = outer_sum(normed_one_low, low_value_one)
    sum_value_bias = jnp.sum(low_value_one.astype(jnp.float32), axis=0)
    grad_normed_one = (
        back_product(low_query_one, query_weight)
        + back_product(low_key_one, key_weight)
        + back_product(low_value_one, value_weight)
    )
    part_zero, sum_self_gain, sum_self_shift = norm_one_back(grad_normed_one)
    tokens_gradient = (
        (grad_one + part_zero).astype(jnp.bfloat16).reshape(seq_count, length, model_width)
    )
    totals = lax.psum(
        (
            sum_self_gain,
            sum_self_shift,
            sum_query_weight,
            sum_query_bias,
            sum_key_weight,
            sum_value_weight,
            sum_value_bias,
            sum_position_table,
            sum_head_scale,
            sum_output_weight,
            sum_output_bias,
            sum_cross_gain,
            sum_cross_shift,
            sum_cross_query,
            sum_cross_query_bias,
            sum_cross_key,
            sum_cross_value,
            sum_cross_value_bias,
            sum_post_gain,
            sum_post_shift,
            sum_cross_output,
            sum_cross_output_bias,
            sum_feed_gain,
            sum_feed_shift,
            sum_inner_weight,
            sum_inner_bias,
            sum_inner_gain,
            sum_inner_shift,
            sum_outer_weight,
            sum_outer_bias,
        ),
        ("dp", "rep"),
    )
    return (layer_output, tokens_gradient, memory_gradient) + tuple(totals)


def solution(mesh):
    in_specs = (
        P(("dp", "rep"), None, None),
        P(("dp", "rep"), None, None),
        P(("dp", "rep")),
        P(("dp", "rep"), None),
        P(("dp", "rep")),
        P(),
        P(None, "rep", "dp", None),
        P(),
        P(),
        P(),
        P(),
        P(),
        P(),
        P(),
        P(),
        P(),
        P(),
        P(),
        P(),
        P(),
        P(),
        P(),
        P(),
        P(),
        P(),
        P(),
        P(),
        P(),
        P(),
        P(),
        P(),
        P(),
        P(),
        P(),
        P(),
        P(),
        P(),
    )
    out_specs = (
        P(("dp", "rep"), None, None),
        P(("dp", "rep"), None, None),
        P(None, "rep", "dp", None),
        P(),
        P(),
        P(),
        P(),
        P(),
        P(),
        P(),
        P(),
        P(),
        P(),
        P(),
        P(),
        P(),
        P(),
        P(),
        P(),
        P(),
        P(),
        P(),
        P(),
        P(),
        P(),
        P(),
        P(),
        P(),
        P(),
        P(),
        P(),
        P(),
        P(),
    )
    return jax.shard_map(local, mesh=mesh, in_specs=in_specs, out_specs=out_specs, check_vma=False)
```

profile of v0, /device:TPU:10, one launch (start us, length us, event | category | flops | bytes accessed | tf_op | source)
XLA Modules:
  0.0 1247.0 jit_solution(17681116033645077815)
XLA Ops:
  7.2 6.8 convolution_convert_fusion
  14.0 6.3 all-to-all-start
  51.6 77.0 %while.86 = (s32[]{:T(128)}, f32[4,8,64,256]{3,1,2,0:T(8,128)}, s32[4,64,256]{2,1,0:T(8,128)}, f32[511,8]{0,1:T(8,128)S(1)}) while((s32[]{:T(128)}, f32[4,8,64,256]{3,1,2,0:T(8,128)}, s32[4,64,256]{2,1,0:T(8,128)}, f32[511,8]{0,1:T(8,128)S(1)}) %tuple.235), condition=%wide.region_3.4_spmd.clone.clone, body=%wide.region_2.3_spmd.clone.sunk.clone | while | flops 812105728 | bytes 737817 | solution.py:155
  52.5 18.4 %fusion.310 = f32[4,8,64,256]{3,1,2,0:T(8,128)} fusion(f32[4,8,64,256]{3,1,2,0:T(8,128)} %get-tuple-element.1226, s32[]{:T(128)} %get-tuple-element.1225, s32[64,256]{1,0:T(8,128)S(1)} %dynamic-slice_bitcast_fusion.18, f32[511,8]{0,1:T(8,128)S(1)} %get-tuple-element.1232), kind=kOutput, calls=%fused_computation.10.clone.1.clone | convolution fusion | flops 812105728 | bytes 606688 | tf_op jit(solution)/shard_map/while/body/eval_jaxpr/qkb,bh->hqk/dot_general | solution.py:153
  71.7 18.4 %fusion.310 = f32[4,8,64,256]{3,1,2,0:T(8,128)} fusion(f32[4,8,64,256]{3,1,2,0:T(8,128)} %get-tuple-element.1226, s32[]{:T(128)} %get-tuple-element.1225, s32[64,256]{1,0:T(8,128)S(1)} %dynamic-slice_bitcast_fusion.18, f32[511,8]{0,1:T(8,128)S(1)} %get-tuple-element.1232), kind=kOutput, calls=%fused_computation.10.clone.1.clone | convolution fusion | flops 812105728 | bytes 606688 | tf_op jit(solution)/shard_map/while/body/eval_jaxpr/qkb,bh->hqk/dot_general | solution.py:153
  91.0 18.4 %fusion.310 = f32[4,8,64,256]{3,1,2,0:T(8,128)} fusion(f32[4,8,64,256]{3,1,2,0:T(8,128)} %get-tuple-element.1226, s32[]{:T(128)} %get-tuple-element.1225, s32[64,256]{1,0:T(8,128)S(1)} %dynamic-slice_bitcast_fusion.18, f32[511,8]{0,1:T(8,128)S(1)} %get-tuple-element.1232), kind=kOutput, calls=%fused_computation.10.clone.1.clone | convolution fusion | flops 812105728 | bytes 606688 | tf_op jit(solution)/shard_map/while/body/eval_jaxpr/qkb,bh->hqk/dot_general | solution.py:153
  110.2 18.4 %fusion.310 = f32[4,8,64,256]{3,1,2,0:T(8,128)} fusion(f32[4,8,64,256]{3,1,2,0:T(8,128)} %get-tuple-element.1226, s32[]{:T(128)} %get-tuple-element.1225, s32[64,256]{1,0:T(8,128)S(1)} %dynamic-slice_bitcast_fusion.18, f32[511,8]{0,1:T(8,128)S(1)} %get-tuple-element.1232), kind=kOutput, calls=%fused_computation.10.clone.1.clone | convolution fusion | flops 812105728 | bytes 606688 | tf_op jit(solution)/shard_map/while/body/eval_jaxpr/qkb,bh->hqk/dot_general | solution.py:153
  131.7 6.7 add_convert_fusion.2
  138.3 6.3 all-to-all-start.1
  144.6 37.2 %while.87 = (s32[]{:T(128)}, f32[8,4,256,64]{2,1,3,0:T(4,128)}, f32[8,4,256]{2,1,0:T(4,128)S(1)}, bf16[8,4,256,64]{2,3,1,0:T(8,128)(2,1)}, bf16[8,4,256,64]{2,3,...) while((s32[]{:T(128)}, f32[8,4,256,64]{2,1,3,0:T(4,128)}, ...), condition=%wide.region_7.8_spmd.clone.clone, body=%wide.region_4.7_spmd.clone.sunk.clone | while | flops 69467136 | bytes 5213285 | solution.py:165
  201.2 7.6 copy.149
  208.7 7.3 reshape_reshape.6
  216.0 4.9 copy.152
  220.9 12.9 %all-to-all-done.1 = bf16[8,4,128,512]{3,2,1,0:T(8,128)(2,1)} async-done(((bf16[8,4,128,512]{3,2,1,0:T(8,128)(2,1)}), bf16[8,4,128,512]{3,2,1,0:T(8,128)(2,1)}, u32[]{:S(2)}, u32[]{:S(2)}) %all-to-all-start.1) | async-done | bytes 4194336 | tf_op jit(solution)/shard_map/all_to_all | solution.py:136
  233.9 7.6 copy.150
  241.4 7.3 reshape_reshape.7
  248.7 4.9 copy.153
  253.6 46.8 %while.88 = (s32[]{:T(128)}, f32[8,4,256,64]{2,3,1,0:T(8,128)}, f32[8,4,256]{2,1,0:T(4,128)S(1)}, bf16[8,4,256,64]{2,3,1,0:T(8,128)(2,1)S(1)}, bf16[8,4,1024,64]...) while((s32[]{:T(128)}, f32[8,4,256,64]{2,3,1,0:T(8,128)}, ...), condition=%wide.region_13.14_spmd.clone.clone, body=%wide.region_10.13_spmd.clone.sunk.clone | while | flops 277875712 | bytes 14076001 | solution.py:180
  308.0 5.2 reshape.568
  317.3 23.2 %fusion.182 = (f32[1024]{0:T(1024)S(1)}, f32[1024,2048]{1,0:T(8,128)S(1)}, f32[1024,2048]{1,0:T(8,128)}, f32[1024,2048]{1,0:T(8,128)}) fusion(f32[2048]{0:T(1024)S(1)} %copy-done.107, bf16[512,2048]{1,0:T(8,128)(2,1)S(1)} %copy-done, f32[1024,512]{1,0:T(8,128)S(1)} %get-tuple-element.785, f32[512]{0:T(512)S(1)} %copy-done.100, f32[512]{0:T(512)S(1)} %copy-done.91, ...), kind=kOutput, calls=%fused_computation.288 | convolution fusion | flops 2288516096 | bytes 29384704 | tf_op jit(solution)/shard_map/dot_general | solution.py:20
  349.5 13.5 %fusion.176 = (f32[2048]{0:T(1024)}, bf16[1024,2048]{1,0:T(8,128)(2,1)S(1)}, bf16[1024,2048]{1,0:T(8,128)(2,1)}) fusion(f32[1024,2048]{1,0:T(8,128)} %get-tuple-element.756, f32[1024]{0:T(1024)} %negate_multiply_fusion.5, f32[1024]{0:T(1024)S(1)} %get-tuple-element.776, f32[1024,2048]{1,0:T(8,128)S(1)} %get-tuple-element.755, ...), kind=kLoop, calls=%fused_computation.282 | loop fusion | flops 56621056 | bytes 41992192 | tf_op jit(solution)/shard_map/reduce_sum | solution.py:203
  363.0 6.6 multiply_reduce_fusion.5
  379.8 89.8 %while.89 = (s32[]{:T(128)}, bf16[8,4,256,64]{2,3,1,0:T(8,128)(2,1)S(1)}, bf16[8,4,1024,64]{2,3,0,1:T(8,128)(2,1)}, bf16[8,4,1024,64]{2,3,0,1:T(8,128)(2,1)}, bf...) while((s32[]{:T(128)}, ...), condition=%wide.region_28.29_spmd.clone.clone, body=%wide.region_26.28_spmd.clone.sunk.clone | while | flops 683674624 | bytes 36225148 | solution.py:219
  469.6 8.2 copy.172
  477.8 8.1 all-to-all-start.2
  504.9 7.8 copy.176
  517.5 57.6 %all-to-all-done.2 = bf16[1,4,1024,512]{3,1,0,2:T(4,128)(2,1)} async-done(((bf16[1,4,1024,512]{3,1,0,2:T(4,128)(2,1)}), bf16[1,4,1024,512]{3,1,0,2:T(4,128)(2,1)}, u32[]{:S(2)}, u32[]{:S(2)}) %all-to-all-start.2) | async-done | bytes 4194336 | tf_op jit(solution)/shard_map/all_to_all | solution.py:229
  575.1 7.8 all-to-all-start.3
  583.0 138.2 %while.90 = (s32[]{:T(128)}, bf16[8,4,256,64]{2,3,1,0:T(8,128)(2,1)}, bf16[8,4,256,64]{2,3,1,0:T(8,128)(2,1)}, bf16[8,4,256,64]{2,3,1,0:T(8,128)(2,1)}, f32[8,25...) while((s32[]{:T(128)}, ...), condition=%wide.region_34.35_spmd.clone.clone, body=%wide.region_31.34_spmd.clone.sunk.clone | while | flops 170851328 | bytes 12018829 | solution.py:269
  588.8 6.9 dynamic_update_slice.99
  606.0 6.9 dynamic_update_slice.99
  623.2 6.9 dynamic_update_slice.99
  640.4 6.9 dynamic_update_slice.99
  657.7 6.9 dynamic_update_slice.99
  674.9 6.9 dynamic_update_slice.99
  692.1 6.9 dynamic_update_slice.99
  709.3 6.9 dynamic_update_slice.99
  744.3 4.9 fusion.142
  749.1 5.5 fusion.146
  754.7 6.8 fusion.149
  781.5 49.2 %while.91 = (s32[]{:T(128)}, f32[511,8]{0,1:T(8,128)S(1)}, s32[4,64,256]{2,1,0:T(8,128)}, f32[4,8,64,256]{3,1,2,0:T(8,128)}) while((s32[]{:T(128)}, f32[511,8]{0,1:T(8,128)S(1)}, s32[4,64,256]{2,1,0:T(8,128)}, f32[4,8,64,256]{3,1,2,0:T(8,128)}) %tuple.234), condition=%wide.region_49.50_spmd.clone.clone, body=%wide.region_48.49_spmd.clone.sunk.clone | while | flops 812113920 | bytes 754179 | solution.py:284
  782.6 11.3 fusion.341
  794.7 11.3 fusion.341
  806.9 11.4 fusion.341
  819.2 11.3 fusion.341
  836.1 6.8 add_convert_fusion
  842.9 211.1 %all-reduce.7.cloned.1.call-done = (f32[512,512]{1,0:T(8,128)}, f32[512,512]{1,0:T(8,128)}, f32[512,512]{1,0:T(8,128)}, f32[512,512]{1,0:T(8,128)}, f32[512,512]...) async-done(((f32[512,512]{1,0:T(8,128)}, f32[512,512]{1,0:T(8,128)}, ...) | async-done | bytes 16777232 | tf_op jit(solution)/shard_map/psum | solution.py:304
  1057.9 158.2 %all-reduce.5.cloned.1.call-done = (f32[512]{0:T(512)}, f32[512]{0:T(512)}, f32[512]{0:T(512)}, f32[512]{0:T(512)}, f32[511,8]{0,1:T(8,128)}, /*index=5*/f32[8]{...) async-done(((f32[512]{0:T(512)}, f32[512]{0:T(512)}, ...) | async-done | bytes 71696 | tf_op jit(solution)/shard_map/psum | solution.py:304
  (688 shorter events, 446.0 us)
Async XLA Ops:
  7.2 309.7 %copy-start = (bf16[512,2048]{1,0:T(8,128)(2,1)S(1)}, bf16[512,2048]{1,0:T(8,128)(2,1)}, u32[]{:S(2)}) copy-start(bf16[512,2048]{1,0:T(8,128)(2,1)} %param.80) | copy-start | bytes 6291460
  14.0 6.4 copy-start.2
  14.0 124.3 %all-to-all-start = ((bf16[8,4,128,512]{3,2,1,0:T(8,128)(2,1)}), bf16[8,4,128,512]{3,2,1,0:T(8,128)(2,1)}, u32[]{:S(2)}, u32[]{:S(2)}) async-start(bf16[8,4,128,512]{3,2,1,0:T(8,128)(2,1)} %convolution_convert_fusion), calls=%async_computation | async-start | bytes 8388608 | tf_op jit(solution)/shard_map/all_to_all | solution.py:135
  37.5 5.2 copy-start.133
  46.6 5.0 copy-start.131
  138.3 95.5 %all-to-all-start.1 = ((bf16[8,4,128,512]{3,2,1,0:T(8,128)(2,1)}), bf16[8,4,128,512]{3,2,1,0:T(8,128)(2,1)}, u32[]{:S(2)}, u32[]{:S(2)}) async-start(bf16[8,4,128,512]{3,2,1,0:T(8,128)(2,1)} %add_convert_fusion.2), calls=%async_computation.1 | async-start | bytes 8388608 | tf_op jit(solution)/shard_map/all_to_all | solution.py:136
  144.6 37.3 %copy-start.123 = (f32[8]{0:T(128)S(1)}, f32[8]{0:T(128)}, u32[]{:S(2)}) copy-start(f32[8]{0:T(128)} %param.64) | copy-start | bytes 100
  248.7 4.9 copy-start.78
  308.0 5.2 copy-start.96
  308.0 5.2 copy-start.137
  308.0 5.2 copy-start.138
  316.4 24.0 %copy-start.9 = (f32[1024,512]{1,0:T(8,128)}, f32[1024,512]{1,0:T(8,128)S(1)}, u32[]{:S(2)}) copy-start(f32[1024,512]{1,0:T(8,128)S(1)} %get-tuple-element.785) | copy-start | bytes 6291460
  317.3 23.2 %copy-start.41 = (bf16[1024,512]{1,0:T(8,128)(2,1)S(1)}, bf16[1024,512]{1,0:T(8,128)(2,1)}, u32[]{:S(2)}) copy-start(bf16[1024,512]{1,0:T(8,128)(2,1)} %bitcast_convert_fusion) | copy-start | bytes 3145732
  317.3 23.2 %copy-start.90 = (f32[2048]{0:T(1024)S(1)}, f32[2048]{0:T(1024)}, u32[]{:S(2)}) copy-start(f32[2048]{0:T(1024)} %param.82) | copy-start | bytes 24580
  317.3 23.2 %copy-start.127 = (bf16[2048,512]{1,0:T(8,128)(2,1)S(1)}, bf16[2048,512]{1,0:T(8,128)(2,1)}, u32[]{:S(2)}) copy-start(bf16[2048,512]{1,0:T(8,128)(2,1)} %param.84) | copy-start | bytes 6291460
  363.0 6.6 copy-start.7
  363.0 6.6 copy-start.10
  363.0 6.6 copy-start.92
  469.6 22.5 %copy-start.23 = (bf16[8,4,256,64]{2,3,1,0:T(8,128)(2,1)}, bf16[8,4,256,64]{2,3,1,0:T(8,128)(2,1)S(1)}, u32[]{:S(2)}) copy-start(bf16[8,4,256,64]{2,3,1,0:T(8,128)(2,1)S(1)} %get-tuple-element.291) | copy-start | bytes 3145732
  477.8 97.3 %all-to-all-start.2 = ((bf16[1,4,1024,512]{3,1,0,2:T(4,128)(2,1)}), bf16[1,4,1024,512]{3,1,0,2:T(4,128)(2,1)}, u32[]{:S(2)}, u32[]{:S(2)}) async-start(bf16[1,4,1024,512]{3,1,0,2:T(4,128)(2,1)} %copy.172), calls=%async_computation.2 | async-start | bytes 8388608 | tf_op jit(solution)/shard_map/all_to_all | solution.py:229
  485.8 4.8 copy-start.3
  485.9 4.7 copy-start.80
  485.9 4.7 copy-start.82
  485.9 4.7 copy-start.93
  485.9 4.7 copy-start.106
  504.9 7.8 copy-start.124
  517.5 65.5 %copy-start.27 = (pred[256,256]{0,1:T(8,128)(4,1)S(1)}, pred[256,256]{0,1:T(8,128)(4,1)}, u32[]{:S(2)}) copy-start(pred[256,256]{0,1:T(8,128)(4,1)} %copy-done.26) | copy-start | bytes 196612
  517.5 65.5 %copy-start.70 = (pred[4,256]{1,0:T(4,128)(4,1)S(1)}, pred[4,256]{1,0:T(4,128)(4,1)}, u32[]{:S(2)}) copy-start(pred[4,256]{1,0:T(4,128)(4,1)} %copy-done.69) | copy-start | bytes 3076
  575.1 179.6 %all-to-all-start.3 = ((bf16[1,4,1024,512]{3,1,0,2:T(4,128)(2,1)}), bf16[1,4,1024,512]{3,1,0,2:T(4,128)(2,1)}, u32[]{:S(2)}, u32[]{:S(2)}) async-start(bf16[1,4,1024,512]{3,1,0,2:T(4,128)(2,1)} %copy.176), calls=%async_computation.3 | async-start | bytes 8388608 | tf_op jit(solution)/shard_map/all_to_all | solution.py:236
  582.9 471.0 %all-reduce.7.cloned.1.call-start = ((), (), s32[]{:S(2)}) async-start(), calls=%async_computation.5 | async-start | bytes 33554432 | tf_op jit(solution)/shard_map/psum | solution.py:304
  723.8 4.9 copy-start.28
  725.0 5.4 copy-start.32
  726.9 5.2 copy-start.30
  730.4 5.7 copy-start.139
  744.3 4.9 copy-start.126
  761.5 454.7 %all-reduce.5.cloned.1.call-start = ((), (), s32[]{:S(2)}) async-start(), calls=%async_computation.4 | async-start | bytes 144384 | tf_op jit(solution)/shard_map/psum | solution.py:304
  771.0 5.6 copy-start.128
  781.5 49.9 %copy-start.67 = (bf16[512,512]{1,0:T(8,128)(2,1)S(1)}, bf16[512,512]{1,0:T(8,128)(2,1)}, u32[]{:S(2)}) copy-start(bf16[512,512]{1,0:T(8,128)(2,1)} %param.72) | copy-start | bytes 1572868
  1053.9 164.7 %copy-start.51 = (f32[512,512]{1,0:T(8,128)S(1)}, f32[512,512]{1,0:T(8,128)}, u32[]{:S(2)}) copy-start(f32[512,512]{1,0:T(8,128)} %get-tuple-element.1367) | copy-start | bytes 3145732
  1056.6 163.5 %copy-start.50 = (f32[512,512]{1,0:T(8,128)S(1)}, f32[512,512]{1,0:T(8,128)}, u32[]{:S(2)}) copy-start(f32[512,512]{1,0:T(8,128)} %get-tuple-element.1369) | copy-start | bytes 3145732
  1221.2 4.9 copy-start.118
  1221.2 5.4 copy-start.47
  1223.9 4.9 copy-start.115
  1223.9 5.5 copy-start.114
  1223.9 6.1 copy-start.46
  1226.6 4.9 copy-start.112
  1226.6 5.5 copy-start.111
  1226.6 6.0 copy-start.35
  (100 other events, 230.6 us)
Sparse Core Ops, SparseCore 0:
  761.6 292.2 all-reduce.6
  1063.2 152.8 all-reduce.4
where the time goes:
time: 1260 us; the launch traced here: 1250 us
  waiting for transfers between devices  440 us (35%)
  matrix products  425 us (34%)
  local copies, waits for them, and re-layouts  266 us (21%)
  other arithmetic  70.4 us (6%)
  starting transfers between devices  28.6 us (2%)
  between operations  15.7 us (1%)
    psum x2, waiting for transfers between devices, local(): lax.psum((sum_self_gain, sum_self_shift, sum_query_weight, sum_query_bias...  369 us
    unnamed x333, local copies, waits for them, and re-layouts  73.7 us
    dot_general x4, matrix products, bias_rows(): jnp.einsum('qkb,bh->hqk', one_hot, position_table, precision=lax.Precisio...  73.6 us
    all_to_all x1, waiting for transfers between devices, local(): lax.all_to_all(low_key_two.reshape(1, seq_count, mem_total, model_width),...  57.6 us
    dynamic_update_slice x16, local copies, waits for them, and re-layouts, local(): lax.map(self_backward, (heads_query, heads_key, heads_value, bias_heads,...  56.4 us
    dot_general x32, matrix products, scores_of(): jnp.einsum('sqd,skd->sqk', query_block, key_block, preferred_element_type...  53.1 us
    dot_general x10, matrix products, matmul(): return jnp.dot(left_side, right_side, preferred_element_type=jnp.float32)  50.8 us
    dot_general x4, matrix products, bucket_sums(): jnp.einsum('qkb,hqk->bh', one_hot, packed[1], precision=lax.Precision.HIG...  45.4 us
  transfers between devices with their start and end apart: 6, of which 4 were waited for; matrix products, arithmetic and copies ran while one was open for 37% of the time, Pallas kernels for 0%

commit v1 on v0

--- a/solution.py
+++ b/solution.py
@@ -302,39 +302,42 @@
         (grad_one + part_zero).astype(jnp.bfloat16).reshape(seq_count, length, model_width)
     )
     totals = lax.psum(
-        (
-            sum_self_gain,
-            sum_self_shift,
-            sum_query_weight,
-            sum_query_bias,
-            sum_key_weight,
-            sum_value_weight,
-            sum_value_bias,
-            sum_position_table,
-            sum_head_scale,
-            sum_output_weight,
-            sum_output_bias,
-            sum_cross_gain,
-            sum_cross_shift,
-            sum_cross_query,
-            sum_cross_query_bias,
-            sum_cross_key,
-            sum_cross_value,
-            sum_cross_value_bias,
-            sum_post_gain,
-            sum_post_shift,
-            sum_cross_output,
-            sum_cross_output_bias,
-            sum_feed_gain,
-            sum_feed_shift,
-            sum_inner_weight,
-            sum_inner_bias,
-            sum_inner_gain,
-            sum_inner_shift,
-            sum_outer_weight,
-            sum_outer_bias,
+        lax.psum(
+            (
+                sum_self_gain,
+                sum_self_shift,
+                sum_query_weight,
+                sum_query_bias,
+                sum_key_weight,
+                sum_value_weight,
+                sum_value_bias,
+                sum_position_table,
+                sum_head_scale,
+                sum_output_weight,
+                sum_output_bias,
+                sum_cross_gain,
+                sum_cross_shift,
+                sum_cross_query,
+                sum_cross_query_bias,
+                sum_cross_key,
+                sum_cross_value,
+                sum_cross_value_bias,
+                sum_post_gain,
+                sum_post_shift,
+                sum_cross_output,
+                sum_cross_output_bias,
+                sum_feed_gain,
+                sum_feed_shift,
+                sum_inner_weight,
+                sum_inner_bias,
+                sum_inner_gain,
+                sum_inner_shift,
+                sum_outer_weight,
+                sum_outer_bias,
+            ),
+            "rep",
         ),
-        ("dp", "rep"),
+        "dp",
     )
     return (layer_output, tokens_gradient, memory_gradient) + tuple(totals)
 

time: 1260 us -> 1750 us (1.39)
  waiting for transfers between devices: 440 us -> 926 us
    psum x0 -> x2, waiting for transfers between devices: none -> 595 us  [local(): lax.psum(lax.psum((sum_self_gain, sum_self_shift, sum_query_weight, sum_q...]
    psum x2, waiting for transfers between devices: 369 us -> 260 us  [local(): lax.psum((sum_self_gain, sum_self_shift, sum_query_weight, sum_query_bias...]
    unnamed x333 -> x331, local copies, waits for them, and re-layouts: 73.7 us -> 73.9 us
  transfers between devices with their start and end apart: 6 -> 8, of which waited for: 4 -> 6; matrix products, arithmetic and copies ran while one was open for 37% -> 27% of each run, Pallas kernels for 0% -> 0%
where the time goes in v1:
time: 1750 us; the launch traced here: 1740 us
  waiting for transfers between devices  926 us (53%)
  matrix products  426 us (24%)
  local copies, waits for them, and re-layouts  265 us (15%)
  other arithmetic  73.5 us (4%)
  starting transfers between devices  28.6 us (2%)
    psum x2, waiting for transfers between devices, local(): lax.psum(lax.psum((sum_self_gain, sum_self_shift, sum_query_weight, sum_q...  595 us
    psum x2, waiting for transfers between devices, local(): lax.psum((sum_self_gain, sum_self_shift, sum_query_weight, sum_query_bias...  260 us
    unnamed x331, local copies, waits for them, and re-layouts  73.9 us
    dot_general x4, matrix products, bias_rows(): jnp.einsum('qkb,bh->hqk', one_hot, position_table, precision=lax.Precisio...  73.6 us
    all_to_all x1, waiting for transfers between devices, local(): lax.all_to_all(low_key_two.reshape(1, seq_count, mem_total, model_width),...  57.8 us
    dynamic_update_slice x16, local copies, waits for them, and re-layouts, local(): lax.map(self_backward, (heads_query, heads_key, heads_value, bias_heads,...  56.3 us
    dot_general x32, matrix products, scores_of(): jnp.einsum('sqd,skd->sqk', query_block, key_block, preferred_element_type...  53.1 us
    dot_general x10, matrix products, matmul(): return jnp.dot(left_side, right_side, preferred_element_type=jnp.float32)  52.4 us
  transfers between devices with their start and end apart: 8, of which 6 were waited for; matrix products, arithmetic and copies ran while one was open for 27% of the time, Pallas kernels for 0%

profile of v1, /device:TPU:10, one launch (start us, length us, event | category | flops | bytes accessed | tf_op | source)
XLA Modules:
  0.0 1735.6 jit_solution(18234448428807387149)
XLA Ops:
  7.2 6.8 convolution_convert_fusion
  14.0 6.3 all-to-all-start
  51.6 77.0 %while.86 = (s32[]{:T(128)}, f32[4,8,64,256]{3,1,2,0:T(8,128)}, s32[4,64,256]{2,1,0:T(8,128)}, f32[511,8]{0,1:T(8,128)S(1)}) while((s32[]{:T(128)}, f32[4,8,64,256]{3,1,2,0:T(8,128)}, s32[4,64,256]{2,1,0:T(8,128)}, f32[511,8]{0,1:T(8,128)S(1)}) %tuple.241), condition=%wide.region_3.4_spmd.clone.clone, body=%wide.region_2.3_spmd.clone.sunk.clone | while | flops 812105728 | bytes 737817 | solution.py:155
  52.5 18.4 %fusion.310 = f32[4,8,64,256]{3,1,2,0:T(8,128)} fusion(f32[4,8,64,256]{3,1,2,0:T(8,128)} %get-tuple-element.1256, s32[]{:T(128)} %get-tuple-element.1255, s32[64,256]{1,0:T(8,128)S(1)} %dynamic-slice_bitcast_fusion.18, f32[511,8]{0,1:T(8,128)S(1)} %get-tuple-element.1262), kind=kOutput, calls=%fused_computation.10.clone.1.clone | convolution fusion | flops 812105728 | bytes 606688 | tf_op jit(solution)/shard_map/while/body/eval_jaxpr/qkb,bh->hqk/dot_general | solution.py:153
  71.7 18.4 %fusion.310 = f32[4,8,64,256]{3,1,2,0:T(8,128)} fusion(f32[4,8,64,256]{3,1,2,0:T(8,128)} %get-tuple-element.1256, s32[]{:T(128)} %get-tuple-element.1255, s32[64,256]{1,0:T(8,128)S(1)} %dynamic-slice_bitcast_fusion.18, f32[511,8]{0,1:T(8,128)S(1)} %get-tuple-element.1262), kind=kOutput, calls=%fused_computation.10.clone.1.clone | convolution fusion | flops 812105728 | bytes 606688 | tf_op jit(solution)/shard_map/while/body/eval_jaxpr/qkb,bh->hqk/dot_general | solution.py:153
  91.0 18.4 %fusion.310 = f32[4,8,64,256]{3,1,2,0:T(8,128)} fusion(f32[4,8,64,256]{3,1,2,0:T(8,128)} %get-tuple-element.1256, s32[]{:T(128)} %get-tuple-element.1255, s32[64,256]{1,0:T(8,128)S(1)} %dynamic-slice_bitcast_fusion.18, f32[511,8]{0,1:T(8,128)S(1)} %get-tuple-element.1262), kind=kOutput, calls=%fused_computation.10.clone.1.clone | convolution fusion | flops 812105728 | bytes 606688 | tf_op jit(solution)/shard_map/while/body/eval_jaxpr/qkb,bh->hqk/dot_general | solution.py:153
  110.2 18.4 %fusion.310 = f32[4,8,64,256]{3,1,2,0:T(8,128)} fusion(f32[4,8,64,256]{3,1,2,0:T(8,128)} %get-tuple-element.1256, s32[]{:T(128)} %get-tuple-element.1255, s32[64,256]{1,0:T(8,128)S(1)} %dynamic-slice_bitcast_fusion.18, f32[511,8]{0,1:T(8,128)S(1)} %get-tuple-element.1262), kind=kOutput, calls=%fused_computation.10.clone.1.clone | convolution fusion | flops 812105728 | bytes 606688 | tf_op jit(solution)/shard_map/while/body/eval_jaxpr/qkb,bh->hqk/dot_general | solution.py:153
  131.6 6.7 add_convert_fusion.2
  138.3 6.3 all-to-all-start.1
  144.6 37.2 %while.87 = (s32[]{:T(128)}, f32[8,4,256,64]{2,1,3,0:T(4,128)}, f32[8,4,256]{2,1,0:T(4,128)S(1)}, bf16[8,4,256,64]{2,3,1,0:T(8,128)(2,1)}, bf16[8,4,256,64]{2,3,...) while((s32[]{:T(128)}, f32[8,4,256,64]{2,1,3,0:T(4,128)}, ...), condition=%wide.region_7.8_spmd.clone.clone, body=%wide.region_4.7_spmd.clone.sunk.clone | while | flops 69467136 | bytes 5213285 | solution.py:165
  201.1 7.6 copy.149
  208.7 7.3 reshape_reshape.6
  220.8 13.0 all-to-all-done.1
  233.8 7.6 copy.150
  241.4 7.3 reshape_reshape.7
  253.6 46.8 %while.88 = (s32[]{:T(128)}, f32[8,4,256,64]{2,3,1,0:T(8,128)}, f32[8,4,256]{2,1,0:T(4,128)S(1)}, bf16[8,4,256,64]{2,3,1,0:T(8,128)(2,1)S(1)}, bf16[8,4,1024,64]...) while((s32[]{:T(128)}, f32[8,4,256,64]{2,3,1,0:T(8,128)}, ...), condition=%wide.region_13.14_spmd.clone.clone, body=%wide.region_10.13_spmd.clone.sunk.clone | while | flops 277875712 | bytes 14076001 | solution.py:180
  307.9 5.2 reshape.568
  317.2 23.2 %fusion.182 = (f32[1024]{0:T(1024)S(1)}, f32[1024,2048]{1,0:T(8,128)S(1)}, f32[1024,2048]{1,0:T(8,128)}, f32[1024,2048]{1,0:T(8,128)}) fusion(f32[2048]{0:T(1024)S(1)} %copy-done.107, bf16[512,2048]{1,0:T(8,128)(2,1)S(1)} %copy-done, f32[1024,512]{1,0:T(8,128)S(1)} %get-tuple-element.815, f32[512]{0:T(512)S(1)} %copy-done.100, f32[512]{0:T(512)S(1)} %copy-done.91, ...), kind=kOutput, calls=%fused_computation.288 | convolution fusion | flops 2288516096 | bytes 29384704 | tf_op jit(solution)/shard_map/dot_general | solution.py:20
  349.4 13.5 fusion.176
  363.0 6.6 multiply_reduce_fusion.5
  379.9 89.5 %while.89 = (s32[]{:T(128)}, bf16[8,4,256,64]{2,3,1,0:T(8,128)(2,1)S(1)}, bf16[8,4,1024,64]{2,3,0,1:T(8,128)(2,1)}, bf16[8,4,1024,64]{2,3,0,1:T(8,128)(2,1)}, bf...) while((s32[]{:T(128)}, ...), condition=%wide.region_28.29_spmd.clone.clone, body=%wide.region_26.28_spmd.clone.sunk.clone | while | flops 683674624 | bytes 36225148 | solution.py:219
  469.4 8.2 copy.172
  477.6 8.1 all-to-all-start.2
  504.7 7.8 copy.176
  517.1 57.8 %all-to-all-done.2 = bf16[1,4,1024,512]{3,1,0,2:T(4,128)(2,1)} async-done(((bf16[1,4,1024,512]{3,1,0,2:T(4,128)(2,1)}), bf16[1,4,1024,512]{3,1,0,2:T(4,128)(2,1)}, u32[]{:S(2)}, u32[]{:S(2)}) %all-to-all-start.2) | async-done | bytes 4194336 | tf_op jit(solution)/shard_map/all_to_all | solution.py:229
  574.9 7.8 all-to-all-start.3
  582.7 138.1 %while.90 = (s32[]{:T(128)}, bf16[8,4,256,64]{2,3,1,0:T(8,128)(2,1)}, bf16[8,4,256,64]{2,3,1,0:T(8,128)(2,1)}, bf16[8,4,256,64]{2,3,1,0:T(8,128)(2,1)}, f32[8,25...) while((s32[]{:T(128)}, ...), condition=%wide.region_34.35_spmd.clone.clone, body=%wide.region_31.34_spmd.clone.sunk.clone | while | flops 170851328 | bytes 12018829 | solution.py:269
  588.5 6.9 dynamic_update_slice.99
  605.7 6.9 dynamic_update_slice.99
  622.9 6.9 dynamic_update_slice.99
  640.1 6.9 dynamic_update_slice.99
  657.3 6.9 dynamic_update_slice.99
  674.5 6.9 dynamic_update_slice.99
  691.8 6.9 dynamic_update_slice.99
  709.0 6.9 dynamic_update_slice.99
  748.7 5.5 fusion.146
  754.3 6.8 fusion.149
  775.8 48.7 %while.91 = (s32[]{:T(128)}, f32[511,8]{0,1:T(8,128)S(1)}, s32[4,64,256]{2,1,0:T(8,128)}, f32[4,8,64,256]{3,1,2,0:T(8,128)}) while((s32[]{:T(128)}, f32[511,8]{0,1:T(8,128)S(1)}, s32[4,64,256]{2,1,0:T(8,128)}, f32[4,8,64,256]{3,1,2,0:T(8,128)}) %tuple.240), condition=%wide.region_56.57_spmd.clone.clone, body=%wide.region_55.56_spmd.clone.sunk.clone | while | flops 812113920 | bytes 754179 | solution.py:284
  776.7 11.3 fusion.341
  788.8 11.3 fusion.341
  801.0 11.3 fusion.341
  813.2 11.3 fusion.341
  825.2 230.1 %all-reduce.15.cloned.1.call-done = (f32[512,512]{1,0:T(8,128)}, f32[512,512]{1,0:T(8,128)}, f32[512,512]{1,0:T(8,128)}, f32[512,512]{1,0:T(8,128)}, f32[512,512...) async-done(((f32[512,512]{1,0:T(8,128)}, f32[512,512]{1,0:T(8,128)}, ...) | async-done | bytes 16777232 | tf_op jit(solution)/shard_map/psum | solution.py:305
  1059.8 5.0 add_convert_fusion.5
  1064.8 30.1 %all-reduce.13.cloned.1.call-done = (f32[512]{0:T(512)}, f32[512]{0:T(512)}, f32[512]{0:T(512)}, f32[512]{0:T(512)}, f32[511,8]{0,1:T(8,128)}, /*index=5*/f32[8]...) async-done(((f32[512]{0:T(512)}, f32[512]{0:T(512)}, ...) | async-done | bytes 71696 | tf_op jit(solution)/shard_map/psum | solution.py:305
  1099.6 6.7 add_convert_fusion
  1106.3 514.2 %all-reduce.11.cloned.1.call-done = (f32[512,512]{1,0:T(8,128)}, f32[512,512]{1,0:T(8,128)}, f32[512,512]{1,0:T(8,128)}, f32[512,512]{1,0:T(8,128)}, f32[512,512...) async-done(((f32[512,512]{1,0:T(8,128)}, f32[512,512]{1,0:T(8,128)}, ...) | async-done | bytes 16777232 | tf_op jit(solution)/shard_map/psum | solution.py:304
  1624.5 80.5 %all-reduce.9.cloned.1.call-done = (f32[512]{0:T(512)}, f32[512]{0:T(512)}, f32[512]{0:T(512)}, f32[512]{0:T(512)}, f32[511,8]{0,1:T(8,128)}, /*index=5*/f32[8]{...) async-done(((f32[512]{0:T(512)}, f32[512]{0:T(512)}, ...) | async-done | bytes 71696 | tf_op jit(solution)/shard_map/psum | solution.py:304
  (692 shorter events, 459.5 us)
Async XLA Ops:
  7.2 309.7 %copy-start = (bf16[512,2048]{1,0:T(8,128)(2,1)S(1)}, bf16[512,2048]{1,0:T(8,128)(2,1)}, u32[]{:S(2)}) copy-start(bf16[512,2048]{1,0:T(8,128)(2,1)} %param.80) | copy-start | bytes 6291460
  14.0 6.4 copy-start.2
  14.0 124.2 %all-to-all-start = ((bf16[8,4,128,512]{3,2,1,0:T(8,128)(2,1)}), bf16[8,4,128,512]{3,2,1,0:T(8,128)(2,1)}, u32[]{:S(2)}, u32[]{:S(2)}) async-start(bf16[8,4,128,512]{3,2,1,0:T(8,128)(2,1)} %convolution_convert_fusion), calls=%async_computation | async-start | bytes 8388608 | tf_op jit(solution)/shard_map/all_to_all | solution.py:135
  37.5 5.2 copy-start.132
  46.6 5.0 copy-start.130
  138.3 95.6 %all-to-all-start.1 = ((bf16[8,4,128,512]{3,2,1,0:T(8,128)(2,1)}), bf16[8,4,128,512]{3,2,1,0:T(8,128)(2,1)}, u32[]{:S(2)}, u32[]{:S(2)}) async-start(bf16[8,4,128,512]{3,2,1,0:T(8,128)(2,1)} %add_convert_fusion.2), calls=%async_computation.1 | async-start | bytes 8388608 | tf_op jit(solution)/shard_map/all_to_all | solution.py:136
  144.6 37.3 %copy-start.123 = (f32[8]{0:T(128)S(1)}, f32[8]{0:T(128)}, u32[]{:S(2)}) copy-start(f32[8]{0:T(128)} %param.64) | copy-start | bytes 100
  248.7 4.9 copy-start.78
  307.9 5.2 copy-start.96
  307.9 5.2 copy-start.136
  307.9 5.2 copy-start.137
  316.4 24.0 %copy-start.8 = (f32[1024,512]{1,0:T(8,128)}, f32[1024,512]{1,0:T(8,128)S(1)}, u32[]{:S(2)}) copy-start(f32[1024,512]{1,0:T(8,128)S(1)} %get-tuple-element.815) | copy-start | bytes 6291460
  317.2 23.2 %copy-start.41 = (bf16[1024,512]{1,0:T(8,128)(2,1)S(1)}, bf16[1024,512]{1,0:T(8,128)(2,1)}, u32[]{:S(2)}) copy-start(bf16[1024,512]{1,0:T(8,128)(2,1)} %bitcast_convert_fusion) | copy-start | bytes 3145732
  317.2 23.2 %copy-start.90 = (f32[2048]{0:T(1024)S(1)}, f32[2048]{0:T(1024)}, u32[]{:S(2)}) copy-start(f32[2048]{0:T(1024)} %param.82) | copy-start | bytes 24580
  317.2 23.2 %copy-start.127 = (bf16[2048,512]{1,0:T(8,128)(2,1)S(1)}, bf16[2048,512]{1,0:T(8,128)(2,1)}, u32[]{:S(2)}) copy-start(bf16[2048,512]{1,0:T(8,128)(2,1)} %param.84) | copy-start | bytes 6291460
  363.0 6.6 copy-start.6
  363.0 6.6 copy-start.9
  363.0 6.6 copy-start.92
  469.3 22.5 %copy-start.23 = (bf16[8,4,256,64]{2,3,1,0:T(8,128)(2,1)}, bf16[8,4,256,64]{2,3,1,0:T(8,128)(2,1)S(1)}, u32[]{:S(2)}) copy-start(bf16[8,4,256,64]{2,3,1,0:T(8,128)(2,1)S(1)} %get-tuple-element.291) | copy-start | bytes 3145732
  477.6 97.3 %all-to-all-start.2 = ((bf16[1,4,1024,512]{3,1,0,2:T(4,128)(2,1)}), bf16[1,4,1024,512]{3,1,0,2:T(4,128)(2,1)}, u32[]{:S(2)}, u32[]{:S(2)}) async-start(bf16[1,4,1024,512]{3,1,0,2:T(4,128)(2,1)} %copy.172), calls=%async_computation.2 | async-start | bytes 8388608 | tf_op jit(solution)/shard_map/all_to_all | solution.py:229
  485.6 4.8 copy-start.3
  485.6 4.7 copy-start.80
  485.7 4.7 copy-start.82
  485.7 4.7 copy-start.93
  504.7 7.8 copy-start.124
  517.1 65.6 %copy-start.27 = (pred[256,256]{0,1:T(8,128)(4,1)S(1)}, pred[256,256]{0,1:T(8,128)(4,1)}, u32[]{:S(2)}) copy-start(pred[256,256]{0,1:T(8,128)(4,1)} %copy-done.26) | copy-start | bytes 196612
  517.1 65.6 %copy-start.70 = (pred[4,256]{1,0:T(4,128)(4,1)S(1)}, pred[4,256]{1,0:T(4,128)(4,1)}, u32[]{:S(2)}) copy-start(pred[4,256]{1,0:T(4,128)(4,1)} %copy-done.69) | copy-start | bytes 3076
  574.9 179.4 %all-to-all-start.3 = ((bf16[1,4,1024,512]{3,1,0,2:T(4,128)(2,1)}), bf16[1,4,1024,512]{3,1,0,2:T(4,128)(2,1)}, u32[]{:S(2)}, u32[]{:S(2)}) async-start(bf16[1,4,1024,512]{3,1,0,2:T(4,128)(2,1)} %copy.176), calls=%async_computation.3 | async-start | bytes 8388608 | tf_op jit(solution)/shard_map/all_to_all | solution.py:236
  582.7 472.6 %all-reduce.15.cloned.1.call-start = ((), (), s32[]{:S(2)}) async-start(), calls=%async_computation.7 | async-start | bytes 33554432 | tf_op jit(solution)/shard_map/psum | solution.py:305
  723.4 4.9 copy-start.28
  724.6 5.4 copy-start.32
  726.6 5.2 copy-start.30
  730.0 5.6 copy-start.138
  743.9 4.9 copy-start.126
  761.1 333.8 %all-reduce.13.cloned.1.call-start = ((), (), s32[]{:S(2)}) async-start(), calls=%async_computation.6 | async-start | bytes 144384 | tf_op jit(solution)/shard_map/psum | solution.py:305
  825.1 795.4 %all-reduce.11.cloned.1.call-start = ((), (), s32[]{:S(2)}) async-start(), calls=%async_computation.5 | async-start | bytes 33554432 | tf_op jit(solution)/shard_map/psum | solution.py:304
  1055.3 649.7 %all-reduce.9.cloned.1.call-start = ((), (), s32[]{:S(2)}) async-start(), calls=%async_computation.4 | async-start | bytes 144384 | tf_op jit(solution)/shard_map/psum | solution.py:304
  1059.8 35.1 %copy-start.67 = (bf16[512,512]{1,0:T(8,128)(2,1)S(1)}, bf16[512,512]{1,0:T(8,128)(2,1)}, u32[]{:S(2)}) copy-start(bf16[512,512]{1,0:T(8,128)(2,1)} %param.72) | copy-start | bytes 1572868
  1620.5 87.0 %copy-start.54 = (f32[512,512]{1,0:T(8,128)S(1)}, f32[512,512]{1,0:T(8,128)}, u32[]{:S(2)}) copy-start(f32[512,512]{1,0:T(8,128)} %get-tuple-element.1397) | copy-start | bytes 3145732
  1623.2 85.8 %copy-start.53 = (f32[512,512]{1,0:T(8,128)S(1)}, f32[512,512]{1,0:T(8,128)}, u32[]{:S(2)}) copy-start(f32[512,512]{1,0:T(8,128)} %get-tuple-element.1399) | copy-start | bytes 3145732
  1710.1 4.9 copy-start.118
  1710.1 5.4 copy-start.48
  1712.8 4.9 copy-start.115
  1712.8 5.5 copy-start.114
  1712.8 6.1 copy-start.46
  1715.5 4.9 copy-start.112
  1715.5 5.5 copy-start.111
  1715.5 6.0 copy-start.35
  (101 other events, 238.9 us)
Sparse Core Ops, SparseCore 0:
  761.2 294.0 all-reduce.14
  1062.0 32.8 all-reduce.12
  1102.5 517.9 all-reduce.10
  1627.4 77.5 all-reduce.8
